TPU v7x, 256 devices: a whole 4x4x8 slice. The times are simulated.
256 devices in a mesh: dp: 8 (over y, core), ctx: 32 (over x, z).
Axes of the slice: x: 4, y: 4, z: 8, core: 2. Of those that a mesh axis runs over, the one named last changes fastest.
Arguments:
- queries: bfloat16 [8, 8192, 2560], P('dp', 'ctx'), may hold values from -120 to 120
- global_keys: bfloat16 [8, 8192, 512], P('dp', 'ctx'), may hold values from -5 to 5
- global_values: bfloat16 [8, 8192, 512], P('dp', 'ctx'), may hold values from -6 to 6
- out_grad: bfloat16 [8, 8192, 2560], P('dp', 'ctx'), may hold values from -6 to 6
- query_gain: float32 [2560], replicated, may hold values from 0.5 to 1.5
- doc_start: int32 [8, 64], P('dp', 'ctx'), may hold values from 0 to 63, as said below
Outputs:
- attn_out: bfloat16 [8, 8192, 2560], P('dp', 'ctx')
- query_grad: bfloat16 [8, 8192, 2560], P('dp', 'ctx')
- key_grad: bfloat16 [8, 8192, 512], P('dp', 'ctx')
- value_grad: bfloat16 [8, 8192, 512], P('dp', 'ctx')
- gain_grad: float32 [2560], replicated
Inputs may be any that keep to these rules, and one draw needn't show every extreme that they name: doc_start[g, b] is the first block of block b's document: it is at most b and at least b - 6, never falls along b, and equals b where a document begins; every slab has a document of exactly 7 blocks.
All inputs are finite; a program needn't handle non-finite values.
Results may differ from a plain program's by a relative error of at most 0.017.
The roundings to bfloat16 on the way count: a program that leaves them out, or rounds other values in their place, can miss the bound.
Values may be sent and summed in bfloat16 or wider, within the bound.
No kernel may reach another device: no remote copies, remote signals or barrier semaphores. Data moves between devices by JAX's collectives and lax.ppermute only.
A program may use at most 64 MiB of HBM per device.

v0:
```python
import math
import jax
import jax.numpy as jnp
from jax import lax
from jax.sharding import PartitionSpec as P

HD = 128
BLOCK = 128
REACH = 4


def shifted(value, axis, steps):
    count = lax.axis_size(axis)
    first, last = (max(0, -steps), min(count, count - steps))
    return lax.ppermute(value, axis, [(source, source + steps) for source in range(first, last)])


def head_group(inputs, allowed, factor):
    query_part, key_part, value_part, grad_part = inputs
    scores = (
        jnp.einsum("tgd,wd->gtw", query_part, key_part, preferred_element_type=jnp.float32) * factor
    )
    scores = jnp.where(allowed[None], scores, -jnp.inf)
    row_max = jnp.max(scores, axis=-1, keepdims=True)
    log_total = row_max + jnp.log(jnp.sum(jnp.exp(scores - row_max), axis=-1, keepdims=True))
    weights = jnp.exp(scores - log_total)
    weights_low = weights.astype(jnp.bfloat16)
    result = jnp.einsum(
        "gtw,wd->tgd", weights_low, value_part, preferred_element_type=jnp.float32
    ).astype(jnp.bfloat16)
    inner_sum = jnp.einsum("tgd,tgd->gt", grad_part, result, preferred_element_type=jnp.float32)
    dweights = jnp.einsum("tgd,wd->gtw", grad_part, value_part, preferred_element_type=jnp.float32)
    dscore_low = (weights * (dweights - inner_sum[..., None])).astype(jnp.bfloat16)
    dquery = (
        jnp.einsum("gtw,wd->tgd", dscore_low, key_part, preferred_element_type=jnp.float32) * factor
    )
    dkey = (
        jnp.einsum("gtw,tgd->wd", dscore_low, query_part, preferred_element_type=jnp.float32)
        * factor
    )
    dvalue = jnp.einsum("gtw,tgd->wd", weights_low, grad_part, preferred_element_type=jnp.float32)
    return (result, dquery, dkey, dvalue)


def local(queries, global_keys, global_values, out_grad, query_gain, doc_start):
    row_count = queries.shape[1]
    reach = REACH
    width = reach * row_count
    device = lax.axis_index("ctx")
    query_rows = queries[0]
    key_rows = global_keys[0]
    value_rows = global_values[0]
    grad_rows = out_grad[0]
    kv_count = key_rows.shape[1] // HD
    group_size = query_rows.shape[1] // (kv_count * HD)
    factor = 1.0 / math.sqrt(HD)
    scaled = (query_rows.astype(jnp.float32) * query_gain).astype(jnp.bfloat16)
    key_list = [key_rows]
    value_list = [value_rows]
    for distance in range(1, reach):
        far_keys, far_values = shifted((key_rows, value_rows), "ctx", distance)
        key_list.insert(0, far_keys)
        value_list.insert(0, far_values)
    window_keys = jnp.concatenate(key_list, axis=0)
    window_values = jnp.concatenate(value_list, axis=0)
    first_device = device - (reach - 1)
    query_pos = device * row_count + jnp.arange(row_count, dtype=jnp.int32)
    key_pos = first_device * row_count + jnp.arange(width, dtype=jnp.int32)
    begins = jnp.repeat(doc_start[0], BLOCK) * BLOCK
    allowed = (key_pos[None, :] <= query_pos[:, None]) & (key_pos[None, :] >= begins[:, None])
    query_four = scaled.reshape(row_count, kv_count, group_size, HD).transpose(1, 0, 2, 3)
    grad_four = grad_rows.reshape(row_count, kv_count, group_size, HD).transpose(1, 0, 2, 3)
    key_three = window_keys.reshape(width, kv_count, HD).transpose(1, 0, 2)
    value_three = window_values.reshape(width, kv_count, HD).transpose(1, 0, 2)
    results, dqueries, dkeys, dvalues = lax.map(
        lambda inputs: head_group(inputs, allowed, factor),
        (query_four, key_three, value_three, grad_four),
    )
    attn_out = results.transpose(1, 0, 2, 3).reshape(row_count, -1)
    dscaled = dqueries.transpose(1, 0, 2, 3).reshape(row_count, -1)

    def by_offset(partial_value):
        return partial_value.reshape(kv_count, reach, row_count, HD)[:, ::-1]

    key_offsets = by_offset(dkeys)
    value_offsets = by_offset(dvalues)
    key_total = key_offsets[:, 0]
    value_total = value_offsets[:, 0]
    for distance in range(1, reach):
        got_keys, got_values = shifted(
            (key_offsets[:, distance], value_offsets[:, distance]), "ctx", -distance
        )
        key_total = key_total + got_keys
        value_total = value_total + got_values
    key_grad = key_total.transpose(1, 0, 2).reshape(row_count, -1).astype(jnp.bfloat16)
    value_grad = value_total.transpose(1, 0, 2).reshape(row_count, -1).astype(jnp.bfloat16)
    query_grad = (dscaled * query_gain).astype(jnp.bfloat16)
    gain_term = jnp.sum(dscaled * query_rows.astype(jnp.float32), axis=0)
    gain_grad = lax.psum(gain_term, ("dp", "ctx"))
    return (attn_out[None], query_grad[None], key_grad[None], value_grad[None], gain_grad)


def solution(mesh):
    return jax.shard_map(
        local,
        mesh=mesh,
        in_specs=(
            P("dp", "ctx", None),
            P("dp", "ctx", None),
            P("dp", "ctx", None),
            P("dp", "ctx", None),
            P(),
            P("dp", "ctx"),
        ),
        out_specs=(
            P("dp", "ctx", None),
            P("dp", "ctx", None),
            P("dp", "ctx", None),
            P("dp", "ctx", None),
            P(),
        ),
        check_vma=False,
    )
```

profile of v0, /device:TPU:1, one launch (start us, length us, event | category | flops | bytes accessed | tf_op | source)
XLA Modules:
  0.0 343.3 jit_solution(1276972712751430127)
XLA Ops:
  0.6 1.1 copy.39
  1.7 5.1 %collective-permute-start.5 = (bf16[256,512]{0,1:T(8,128)(2,1)S(1)}, bf16[256,512]{0,1:T(8,128)(2,1)}, u32[]{:S(2)}, u32[]{:S(2)}) collective-permute-start(bf16[256,512]{0,1:T(8,128)(2,1)S(1)} %bitcast.227), channel_id=1, source_target_pairs={{0,1},{1,2},{2,3},{3,4},{4,5},{5,6},{6,7},{7,8},{8,9},{9,10},{10,1... | collective-permute-start | bytes 786440 | tf_op jit(solution)/shard_map/ppermute | solution.py:15
  6.8 4.9 %collective-permute-start.4 = (bf16[256,512]{0,1:T(8,128)(2,1)S(1)}, bf16[256,512]{0,1:T(8,128)(2,1)}, u32[]{:S(2)}, u32[]{:S(2)}) collective-permute-start(bf16[256,512]{0,1:T(8,128)(2,1)S(1)} %bitcast.228), channel_id=1, source_target_pairs={{0,2},{1,3},{2,4},{3,5},{4,6},{5,7},{6,8},{7,9},{8,10},{9,11},{10,... | collective-permute-start | bytes 786440 | tf_op jit(solution)/shard_map/ppermute | solution.py:15
  11.7 5.7 %collective-permute-start.3 = (bf16[256,512]{0,1:T(8,128)(2,1)S(1)}, bf16[256,512]{0,1:T(8,128)(2,1)}, u32[]{:S(2)}, u32[]{:S(2)}) collective-permute-start(bf16[256,512]{0,1:T(8,128)(2,1)S(1)} %bitcast.229), channel_id=1, source_target_pairs={{0,3},{1,4},{2,5},{3,6},{4,7},{5,8},{6,9},{7,10},{8,11},{9,12},{10... | collective-permute-start | bytes 786440 | tf_op jit(solution)/shard_map/ppermute | solution.py:15
  17.4 2.6 collective-permute-start.2
  20.0 2.3 collective-permute-start.1
  23.1 1.6 copy.41
  24.7 1.7 fusion.35
  26.5 17.9 %collective-permute-done.2 = bf16[256,512]{1,0:T(8,128)(2,1)S(1)} collective-permute-done((bf16[256,512]{1,0:T(8,128)(2,1)}, bf16[256,512]{1,0:T(8,128)(2,1)S(1)}, u32[]{:S(2)}, u32[]{:S(2)}) %collective-permute-start.2) | collective-permute-done | bytes 262176 | tf_op jit(solution)/shard_map/ppermute | solution.py:15
  44.5 9.5 %collective-permute-start = (bf16[256,512]{1,0:T(8,128)(2,1)S(1)}, bf16[256,512]{1,0:T(8,128)(2,1)}, u32[]{:S(2)}, u32[]{:S(2)}) collective-permute-start(bf16[256,512]{1,0:T(8,128)(2,1)S(1)} %bitcast.240), channel_id=1, source_target_pairs={{0,3},{1,4},{2,5},{3,6},{4,7},{5,8},{6,9},{7,10},{8,11},{9,12},{10... | collective-permute-start | bytes 786440 | tf_op jit(solution)/shard_map/ppermute | solution.py:15
  54.1 2.5 copy.42
  56.6 1.1 copy.37
  57.7 1.2 copy.36
  58.9 2.2 maximum_bitcast_fusion.1
  61.1 1.1 copy.35
  62.2 1.1 maximum_bitcast_fusion
  63.4 68.0 %while.17 = (s32[]{:T(128)}, bf16[4,256,5,128]{1,3,2,0:T(8,128)(2,1)}, f32[4,256,5,128]{1,3,2,0:T(8,128)}, f32[4,1024,128]{2,1,0:T(8,128)}, f32[4,1024,128]{2,1,...) while((s32[]{:T(128)}, ...), condition=%wide.region_3.4_spmd.clone, body=%wide.region_0.3_spmd.clone.sunk | while | flops 2042689024 | bytes 49229988 | solution.py:75
  63.6 1.0 constant_dynamic-slice_fusion.4
  65.1 2.0 fusion.71
  67.1 1.1 exponential_reduce_fusion.2
  68.4 2.2 bitcast_dynamic-update-slice_fusion.2
  70.7 3.1 fusion.75
  73.8 2.6 fusion.72
  76.4 1.7 fusion.74
  78.1 2.3 fusion.73
  80.6 1.0 constant_dynamic-slice_fusion.4
  82.1 2.0 fusion.71
  84.1 1.1 exponential_reduce_fusion.2
  85.4 2.2 bitcast_dynamic-update-slice_fusion.2
  87.7 3.1 fusion.75
  90.8 2.6 fusion.72
  93.4 1.6 fusion.74
  95.1 2.3 fusion.73
  99.2 2.0 fusion.71
  101.1 1.1 exponential_reduce_fusion.2
  102.4 2.2 bitcast_dynamic-update-slice_fusion.2
  104.7 3.1 fusion.75
  107.8 2.6 fusion.72
  110.4 1.6 fusion.74
  112.1 2.3 fusion.73
  114.7 1.0 constant_dynamic-slice_fusion.4
  116.2 2.0 fusion.71
  118.2 1.1 exponential_reduce_fusion.2
  119.4 2.2 bitcast_dynamic-update-slice_fusion.2
  121.7 3.1 fusion.75
  124.8 2.6 fusion.72
  127.4 1.6 fusion.74
  129.1 2.3 fusion.73
  131.4 1.7 fusion.46
  133.4 1.2 copy.109
  134.9 1.4 collective-permute-start.11
  136.4 1.3 collective-permute-start.9
  137.7 1.5 collective-permute-start.10
  140.1 1.1 copy.112
  141.3 1.1 copy.110
  142.4 1.3 collective-permute-start.8
  143.7 1.3 collective-permute-start.6
  145.0 33.2 %collective-permute-done.11 = f32[4,256,128]{2,0,1:T(4,128)S(1)} collective-permute-done((f32[4,256,128]{2,0,1:T(4,128)S(1)}, f32[4,256,128]{2,0,1:T(4,128)S(1)}, u32[]{:S(2)}, u32[]{:S(2)}) %collective-permute-start.11) | collective-permute-done | bytes 524320 | tf_op jit(solution)/shard_map/ppermute | solution.py:15
  178.2 1.3 collective-permute-start.7
  180.0 2.4 copy.54
  182.4 1.6 copy.55
  184.0 153.9 %psum.7 = f32[2560]{0:T(1024)} all-reduce(f32[2560]{0:T(1024)S(1)} %reduce_sum.21), channel_id=1, replica_groups=mesh['dp'=8,'ctx'=32] {'dp','ctx'}, use_global_device_ids=true, to_apply=%region_5.6 | all-reduce | flops 2560 | bytes 20480 | tf_op jit(solution)/shard_map/psum | solution.py:99
  337.9 1.9 fusion.45
  340.6 1.9 fusion.44
  (82 shorter events, 9.5 us)
Async XLA Ops:
  1.7 57.2 %collective-permute-start.5 = (bf16[256,512]{0,1:T(8,128)(2,1)S(1)}, bf16[256,512]{0,1:T(8,128)(2,1)}, u32[]{:S(2)}, u32[]{:S(2)}) collective-permute-start(bf16[256,512]{0,1:T(8,128)(2,1)S(1)} %bitcast.227), channel_id=1, source_target_pairs={{0,1},{1,2},{2,3},{3,4},{4,5},{5,6},{6,7},{7,8},{8,9},{9,10},{10,1... | collective-permute-start | bytes 786440 | tf_op jit(solution)/shard_map/ppermute | solution.py:15
  6.8 52.1 %collective-permute-start.4 = (bf16[256,512]{0,1:T(8,128)(2,1)S(1)}, bf16[256,512]{0,1:T(8,128)(2,1)}, u32[]{:S(2)}, u32[]{:S(2)}) collective-permute-start(bf16[256,512]{0,1:T(8,128)(2,1)S(1)} %bitcast.228), channel_id=1, source_target_pairs={{0,2},{1,3},{2,4},{3,5},{4,6},{5,7},{6,8},{7,9},{8,10},{9,11},{10,... | collective-permute-start | bytes 786440 | tf_op jit(solution)/shard_map/ppermute | solution.py:15
  11.7 47.2 %collective-permute-start.3 = (bf16[256,512]{0,1:T(8,128)(2,1)S(1)}, bf16[256,512]{0,1:T(8,128)(2,1)}, u32[]{:S(2)}, u32[]{:S(2)}) collective-permute-start(bf16[256,512]{0,1:T(8,128)(2,1)S(1)} %bitcast.229), channel_id=1, source_target_pairs={{0,3},{1,4},{2,5},{3,6},{4,7},{5,8},{6,9},{7,10},{8,11},{9,12},{10... | collective-permute-start | bytes 786440 | tf_op jit(solution)/shard_map/ppermute | solution.py:15
  17.4 27.1 %collective-permute-start.2 = (bf16[256,512]{1,0:T(8,128)(2,1)}, bf16[256,512]{1,0:T(8,128)(2,1)S(1)}, u32[]{:S(2)}, u32[]{:S(2)}) collective-permute-start(bf16[256,512]{1,0:T(8,128)(2,1)} %bitcast.238), channel_id=1, source_target_pairs={{0,1},{1,2},{2,3},{3,4},{4,5},{5,6},{6,7},{7,8},{8,9},{9,10},{10,1... | collective-permute-start | bytes 786440 | tf_op jit(solution)/shard_map/ppermute | solution.py:15
  20.0 37.7 %collective-permute-start.1 = (bf16[256,512]{1,0:T(8,128)(2,1)}, bf16[256,512]{1,0:T(8,128)(2,1)}, u32[]{:S(2)}, u32[]{:S(2)}) collective-permute-start(bf16[256,512]{1,0:T(8,128)(2,1)} %bitcast.239), channel_id=1, source_target_pairs={{0,2},{1,3},{2,4},{3,5},{4,6},{5,7},{6,8},{7,9},{8,10},{9,11},{10,... | collective-permute-start | bytes 786440 | tf_op jit(solution)/shard_map/ppermute | solution.py:15
  24.7 31.9 %copy-start = (f32[1,256,2560]{1,2,0:T(8,128)}, f32[1,256,2560]{1,2,0:T(8,128)S(1)}, u32[]{:S(2)}) copy-start(f32[1,256,2560]{1,2,0:T(8,128)S(1)} %copy.41) | copy-start | bytes 7864324
  24.7 1.8 copy-start.10
  24.7 19.7 %copy-start.7 = (bf16[1,256,512]{2,1,0:T(8,128)(2,1)S(1)}, bf16[1,256,512]{2,1,0:T(8,128)(2,1)}, u32[]{:S(2)}) copy-start(bf16[1,256,512]{2,1,0:T(8,128)(2,1)} %param.10) | copy-start | bytes 786436
  44.5 9.5 %copy-start.8 = (bf16[256,512]{1,0:T(8,128)(2,1)}, bf16[256,512]{1,0:T(8,128)(2,1)S(1)}, u32[]{:S(2)}) copy-start(bf16[256,512]{1,0:T(8,128)(2,1)S(1)} %collective-permute-done.2) | copy-start | bytes 786436
  44.5 16.7 %collective-permute-start = (bf16[256,512]{1,0:T(8,128)(2,1)S(1)}, bf16[256,512]{1,0:T(8,128)(2,1)}, u32[]{:S(2)}, u32[]{:S(2)}) collective-permute-start(bf16[256,512]{1,0:T(8,128)(2,1)S(1)} %bitcast.240), channel_id=1, source_target_pairs={{0,3},{1,4},{2,5},{3,6},{4,7},{5,8},{6,9},{7,10},{8,11},{9,12},{10... | collective-permute-start | bytes 786440 | tf_op jit(solution)/shard_map/ppermute | solution.py:15
  57.7 5.7 %copy-start.2 = (bf16[4,256,5,128]{1,3,2,0:T(8,128)(2,1)S(1)}, bf16[4,256,5,128]{1,3,2,0:T(8,128)(2,1)}, u32[]{:S(2)}) copy-start(bf16[4,256,5,128]{1,3,2,0:T(8,128)(2,1)} %fusion.35) | copy-start | bytes 3932164
  67.1 1.2 copy-start.5
  84.1 1.2 copy-start.5
  101.1 1.2 copy-start.5
  118.2 1.2 copy-start.5
  133.1 6.1 %copy-start.3 = (f32[4,256,5,128]{1,3,2,0:T(8,128)S(1)}, f32[4,256,5,128]{1,3,2,0:T(8,128)}, u32[]{:S(2)}) copy-start(f32[4,256,5,128]{1,3,2,0:T(8,128)} %get-tuple-element.61) | copy-start | bytes 7864324
  133.1 6.1 %copy-start.9 = (f32[2560]{0:T(1024)S(1)}, f32[2560]{0:T(1024)}, u32[]{:S(2)}) copy-start(f32[2560]{0:T(1024)} %param.12) | copy-start | bytes 30724
  134.6 5.0 %copy-start.4 = (f32[4,1024,128]{2,1,0:T(8,128)S(1)}, f32[4,1024,128]{2,1,0:T(8,128)}, u32[]{:S(2)}) copy-start(f32[4,1024,128]{2,1,0:T(8,128)} %get-tuple-element.62) | copy-start | bytes 6291460
  134.9 43.2 %collective-permute-start.11 = (f32[4,256,128]{2,0,1:T(4,128)S(1)}, f32[4,256,128]{2,0,1:T(4,128)S(1)}, u32[]{:S(2)}, u32[]{:S(2)}) collective-permute-start(f32[4,256,128]{2,0,1:T(4,128)S(1)} %bitcast.237), channel_id=1, source_target_pairs={{3,0},{4,1},{5,2},{6,3},{7,4},{8,5},{9,6},{10,7},{11,8},{12,9},{13... | collective-permute-start | bytes 1572872 | tf_op jit(solution)/shard_map/ppermute | solution.py:15
  136.4 201.5 %collective-permute-start.9 = (f32[4,256,128]{2,0,1:T(4,128)}, f32[4,256,128]{2,0,1:T(4,128)}, u32[]{:S(2)}, u32[]{:S(2)}) collective-permute-start(f32[4,256,128]{2,0,1:T(4,128)} %bitcast.170), channel_id=1, source_target_pairs={{1,0},{2,1},{3,2},{4,3},{5,4},{6,5},{7,6},{8,7},{9,8},{10,9},{11,1... | collective-permute-start | bytes 1572872 | tf_op jit(solution)/shard_map/ppermute | solution.py:15
  137.7 200.2 %collective-permute-start.10 = (f32[4,256,128]{2,0,1:T(4,128)S(1)}, f32[4,256,128]{2,0,1:T(4,128)}, u32[]{:S(2)}, u32[]{:S(2)}) collective-permute-start(f32[4,256,128]{2,0,1:T(4,128)S(1)} %bitcast.235), channel_id=1, source_target_pairs={{2,0},{3,1},{4,2},{5,3},{6,4},{7,5},{8,6},{9,7},{10,8},{11,9},{12,... | collective-permute-start | bytes 1572872 | tf_op jit(solution)/shard_map/ppermute | solution.py:15
  139.8 39.7 %copy-start.1 = (f32[1,256,2560]{1,2,0:T(8,128)S(1)}, f32[1,256,2560]{1,2,0:T(8,128)}, u32[]{:S(2)}) copy-start(f32[1,256,2560]{1,2,0:T(8,128)} %copy-done) | copy-start | bytes 7864324
  142.4 198.2 %collective-permute-start.8 = (f32[4,256,128]{2,0,1:T(4,128)}, f32[4,256,128]{2,0,1:T(4,128)}, u32[]{:S(2)}, u32[]{:S(2)}) collective-permute-start(f32[4,256,128]{2,0,1:T(4,128)} %bitcast.171), channel_id=1, source_target_pairs={{3,0},{4,1},{5,2},{6,3},{7,4},{8,5},{9,6},{10,7},{11,8},{12,9},{13... | collective-permute-start | bytes 1572872 | tf_op jit(solution)/shard_map/ppermute | solution.py:15
  143.7 196.9 %collective-permute-start.6 = (f32[4,256,128]{2,0,1:T(4,128)}, f32[4,256,128]{2,0,1:T(4,128)}, u32[]{:S(2)}, u32[]{:S(2)}) collective-permute-start(f32[4,256,128]{2,0,1:T(4,128)} %bitcast.173), channel_id=1, source_target_pairs={{1,0},{2,1},{3,2},{4,3},{5,4},{6,5},{7,6},{8,7},{9,8},{10,9},{11,1... | collective-permute-start | bytes 1572872 | tf_op jit(solution)/shard_map/ppermute | solution.py:15
  178.2 1.3 copy-start.6
  178.2 162.4 %collective-permute-start.7 = (f32[4,256,128]{2,0,1:T(4,128)S(1)}, f32[4,256,128]{2,0,1:T(4,128)}, u32[]{:S(2)}, u32[]{:S(2)}) collective-permute-start(f32[4,256,128]{2,0,1:T(4,128)S(1)} %bitcast.236), channel_id=1, source_target_pairs={{2,0},{3,1},{4,2},{5,3},{6,4},{7,5},{8,6},{9,7},{10,8},{11,9},{12,... | collective-permute-start | bytes 1572872 | tf_op jit(solution)/shard_map/ppermute | solution.py:15
where the time goes:
time: 345 us; the launch traced here: 343 us
  blocking collectives  154 us (45%)
  matrix products  55.5 us (16%)
  waiting for transfers between devices  51.1 us (15%)
  starting transfers between devices  38.2 us (11%)
  local copies, waits for them, and re-layouts  27.5 us (8%)
  other arithmetic  15.8 us (5%)
    psum x1, blocking collectives, local(): gain_grad = lax.psum(gain_term, ('dp', 'ctx'))  154 us
    ppermute x12, waiting for transfers between devices, shifted(): lax.ppermute(value, axis, [(source, source + steps) for source in range(f...  51.1 us
    ppermute x12, starting transfers between devices, shifted(): lax.ppermute(value, axis, [(source, source + steps) for source in range(f...  38.2 us
    dot_general x4, matrix products, head_group(): jnp.einsum('gtw,tgd->wd', weights_low, grad_part, preferred_element_type=...  12.5 us
    unnamed x31, local copies, waits for them, and re-layouts  12.2 us
    dot_general x4, matrix products, head_group(): jnp.einsum('tgd,wd->gtw', grad_part, value_part, preferred_element_type=j...  10.4 us
    dot_general x4, matrix products, head_group(): jnp.einsum('gtw,wd->tgd', dscore_low, key_part, preferred_element_type=jn...  9.25 us
    dot_general x4, matrix products, head_group(): jnp.einsum('gtw,wd->tgd', weights_low, value_part, preferred_element_type...  8.8 us
  transfers between devices with their start and end apart: 12, of which 2 were waited for; matrix products, arithmetic and copies ran while one was open for 6% of the time, Pallas kernels for 0%

commit v1 on v0

--- a/solution.py
+++ b/solution.py
@@ -96,7 +96,9 @@
     value_grad = value_total.transpose(1, 0, 2).reshape(row_count, -1).astype(jnp.bfloat16)
     query_grad = (dscaled * query_gain).astype(jnp.bfloat16)
     gain_term = jnp.sum(dscaled * query_rows.astype(jnp.float32), axis=0)
-    gain_grad = lax.psum(gain_term, ("dp", "ctx"))
+    gain_grad = gain_term
+    for name in ("ctx", "dp"):
+        gain_grad = lax.psum(gain_grad, name)
     return (attn_out[None], query_grad[None], key_grad[None], value_grad[None], gain_grad)
 
 

time: 345 us -> 450 us (1.30)
  blocking collectives: 154 us -> 259 us
    psum x1 -> x2, blocking collectives: 154 us -> 259 us  [local(): gain_grad = lax.psum(gain_grad, name)]
  transfers between devices with their start and end apart: 12 -> 12, of which waited for: 2 -> 2; matrix products, arithmetic and copies ran while one was open for 6% -> 5% of each run, Pallas kernels for 0% -> 0%
where the time goes in v1:
time: 450 us; the launch traced here: 448 us
  blocking collectives  259 us (58%)
  matrix products  55.5 us (12%)
  waiting for transfers between devices  51.1 us (11%)
  starting transfers between devices  38.2 us (8%)
  local copies, waits for them, and re-layouts  27.5 us (6%)
  other arithmetic  15.9 us (4%)
    psum x2, blocking collectives, local(): gain_grad = lax.psum(gain_grad, name)  259 us
    ppermute x12, waiting for transfers between devices, shifted(): lax.ppermute(value, axis, [(source, source + steps) for source in range(f...  51.1 us
    ppermute x12, starting transfers between devices, shifted(): lax.ppermute(value, axis, [(source, source + steps) for source in range(f...  38.2 us
    dot_general x4, matrix products, head_group(): jnp.einsum('gtw,tgd->wd', weights_low, grad_part, preferred_element_type=...  12.6 us
    unnamed x31, local copies, waits for them, and re-layouts  12.2 us
    dot_general x4, matrix products, head_group(): jnp.einsum('tgd,wd->gtw', grad_part, value_part, preferred_element_type=j...  10.4 us
    dot_general x4, matrix products, head_group(): jnp.einsum('gtw,wd->tgd', dscore_low, key_part, preferred_element_type=jn...  9.23 us
  transfers between devices with their start and end apart: 12, of which 2 were waited for; matrix products, arithmetic and copies ran while one was open for 5% of the time, Pallas kernels for 0%

profile of v1, /device:TPU:1, one launch (start us, length us, event | category | flops | bytes accessed | tf_op | source)
XLA Modules:
  0.0 448.1 jit_solution(16250482573742724201)
XLA Ops:
  0.6 1.1 copy.39
  1.7 5.1 %collective-permute-start.5 = (bf16[256,512]{0,1:T(8,128)(2,1)S(1)}, bf16[256,512]{0,1:T(8,128)(2,1)}, u32[]{:S(2)}, u32[]{:S(2)}) collective-permute-start(bf16[256,512]{0,1:T(8,128)(2,1)S(1)} %bitcast.227), channel_id=1, source_target_pairs={{0,1},{1,2},{2,3},{3,4},{4,5},{5,6},{6,7},{7,8},{8,9},{9,10},{10,1... | collective-permute-start | bytes 786440 | tf_op jit(solution)/shard_map/ppermute | solution.py:15
  6.8 4.9 %collective-permute-start.4 = (bf16[256,512]{0,1:T(8,128)(2,1)S(1)}, bf16[256,512]{0,1:T(8,128)(2,1)}, u32[]{:S(2)}, u32[]{:S(2)}) collective-permute-start(bf16[256,512]{0,1:T(8,128)(2,1)S(1)} %bitcast.228), channel_id=1, source_target_pairs={{0,2},{1,3},{2,4},{3,5},{4,6},{5,7},{6,8},{7,9},{8,10},{9,11},{10,... | collective-permute-start | bytes 786440 | tf_op jit(solution)/shard_map/ppermute | solution.py:15
  11.7 5.7 %collective-permute-start.3 = (bf16[256,512]{0,1:T(8,128)(2,1)S(1)}, bf16[256,512]{0,1:T(8,128)(2,1)}, u32[]{:S(2)}, u32[]{:S(2)}) collective-permute-start(bf16[256,512]{0,1:T(8,128)(2,1)S(1)} %bitcast.229), channel_id=1, source_target_pairs={{0,3},{1,4},{2,5},{3,6},{4,7},{5,8},{6,9},{7,10},{8,11},{9,12},{10... | collective-permute-start | bytes 786440 | tf_op jit(solution)/shard_map/ppermute | solution.py:15
  17.4 2.6 collective-permute-start.2
  20.0 2.3 collective-permute-start.1
  23.1 1.6 copy.41
  24.7 1.7 fusion.35
  26.5 17.9 %collective-permute-done.2 = bf16[256,512]{1,0:T(8,128)(2,1)S(1)} collective-permute-done((bf16[256,512]{1,0:T(8,128)(2,1)}, bf16[256,512]{1,0:T(8,128)(2,1)S(1)}, u32[]{:S(2)}, u32[]{:S(2)}) %collective-permute-start.2) | collective-permute-done | bytes 262176 | tf_op jit(solution)/shard_map/ppermute | solution.py:15
  44.5 9.5 %collective-permute-start = (bf16[256,512]{1,0:T(8,128)(2,1)S(1)}, bf16[256,512]{1,0:T(8,128)(2,1)}, u32[]{:S(2)}, u32[]{:S(2)}) collective-permute-start(bf16[256,512]{1,0:T(8,128)(2,1)S(1)} %bitcast.240), channel_id=1, source_target_pairs={{0,3},{1,4},{2,5},{3,6},{4,7},{5,8},{6,9},{7,10},{8,11},{9,12},{10... | collective-permute-start | bytes 786440 | tf_op jit(solution)/shard_map/ppermute | solution.py:15
  54.1 2.5 copy.42
  56.6 1.1 copy.37
  57.7 1.2 copy.36
  58.9 2.2 maximum_bitcast_fusion.1
  61.1 1.1 copy.35
  62.2 1.1 maximum_bitcast_fusion
  63.4 68.1 %while.17 = (s32[]{:T(128)}, bf16[4,256,5,128]{1,3,2,0:T(8,128)(2,1)}, f32[4,256,5,128]{1,3,2,0:T(8,128)}, f32[4,1024,128]{2,1,0:T(8,128)}, f32[4,1024,128]{2,1,...) while((s32[]{:T(128)}, ...), condition=%wide.region_3.4_spmd.clone, body=%wide.region_0.3_spmd.clone.sunk | while | flops 2042689024 | bytes 49229988 | solution.py:75
  65.2 2.0 fusion.71
  67.1 1.1 exponential_reduce_fusion.2
  68.4 2.2 bitcast_dynamic-update-slice_fusion.2
  70.7 3.1 fusion.75
  73.8 2.6 fusion.72
  76.4 1.7 fusion.74
  78.1 2.3 fusion.73
  80.7 1.0 constant_dynamic-slice_fusion.4
  82.2 2.0 fusion.71
  84.1 1.1 exponential_reduce_fusion.2
  85.4 2.2 bitcast_dynamic-update-slice_fusion.2
  87.7 3.2 fusion.75
  90.8 2.6 fusion.72
  93.4 1.6 fusion.74
  95.1 2.3 fusion.73
  97.7 1.0 constant_dynamic-slice_fusion.4
  99.2 2.0 fusion.71
  101.2 1.1 exponential_reduce_fusion.2
  102.4 2.2 bitcast_dynamic-update-slice_fusion.2
  104.7 3.1 fusion.75
  107.9 2.6 fusion.72
  110.5 1.7 fusion.74
  112.1 2.3 fusion.73
  116.2 2.0 fusion.71
  118.2 1.1 exponential_reduce_fusion.2
  119.4 2.2 bitcast_dynamic-update-slice_fusion.2
  121.7 3.2 fusion.75
  124.9 2.6 fusion.72
  127.5 1.7 fusion.74
  129.2 2.3 fusion.73
  131.5 1.7 fusion.46
  133.5 1.2 copy.109
  135.1 1.4 collective-permute-start.11
  136.5 1.3 collective-permute-start.9
  137.8 1.5 collective-permute-start.10
  140.2 1.1 copy.112
  141.4 1.1 copy.110
  142.5 1.3 collective-permute-start.8
  143.8 1.3 collective-permute-start.6
  145.1 33.2 %collective-permute-done.11 = f32[4,256,128]{2,0,1:T(4,128)S(1)} collective-permute-done((f32[4,256,128]{2,0,1:T(4,128)S(1)}, f32[4,256,128]{2,0,1:T(4,128)S(1)}, u32[]{:S(2)}, u32[]{:S(2)}) %collective-permute-start.11) | collective-permute-done | bytes 524320 | tf_op jit(solution)/shard_map/ppermute | solution.py:15
  178.3 1.3 collective-permute-start.7
  180.1 2.4 copy.54
  182.5 1.6 copy.55
  184.1 210.0 %psum.14 = f32[2560]{0:T(1024)S(1)} all-reduce(f32[2560]{0:T(1024)S(1)} %reduce_sum.21), channel_id=1, replica_groups=mesh['dp'=8,'ctx'=32] {'ctx'}, use_global_device_ids=true, to_apply=%region_5.6 | all-reduce | flops 2560 | bytes 20480 | tf_op jit(solution)/shard_map/psum | solution.py:101
  394.1 48.6 %psum.15 = f32[2560]{0:T(1024)} all-reduce(f32[2560]{0:T(1024)S(1)} %psum.14), channel_id=1, replica_groups=mesh['dp'=8,'ctx'=32] {'dp'}, use_global_device_ids=true, to_apply=%region_6.7 | all-reduce | flops 2560 | bytes 20480 | tf_op jit(solution)/shard_map/psum | solution.py:101
  442.7 1.9 fusion.45
  445.4 1.9 fusion.44
  (83 shorter events, 10.5 us)
Async XLA Ops:
  1.7 57.1 %collective-permute-start.5 = (bf16[256,512]{0,1:T(8,128)(2,1)S(1)}, bf16[256,512]{0,1:T(8,128)(2,1)}, u32[]{:S(2)}, u32[]{:S(2)}) collective-permute-start(bf16[256,512]{0,1:T(8,128)(2,1)S(1)} %bitcast.227), channel_id=1, source_target_pairs={{0,1},{1,2},{2,3},{3,4},{4,5},{5,6},{6,7},{7,8},{8,9},{9,10},{10,1... | collective-permute-start | bytes 786440 | tf_op jit(solution)/shard_map/ppermute | solution.py:15
  6.8 52.1 %collective-permute-start.4 = (bf16[256,512]{0,1:T(8,128)(2,1)S(1)}, bf16[256,512]{0,1:T(8,128)(2,1)}, u32[]{:S(2)}, u32[]{:S(2)}) collective-permute-start(bf16[256,512]{0,1:T(8,128)(2,1)S(1)} %bitcast.228), channel_id=1, source_target_pairs={{0,2},{1,3},{2,4},{3,5},{4,6},{5,7},{6,8},{7,9},{8,10},{9,11},{10,... | collective-permute-start | bytes 786440 | tf_op jit(solution)/shard_map/ppermute | solution.py:15
  11.7 47.2 %collective-permute-start.3 = (bf16[256,512]{0,1:T(8,128)(2,1)S(1)}, bf16[256,512]{0,1:T(8,128)(2,1)}, u32[]{:S(2)}, u32[]{:S(2)}) collective-permute-start(bf16[256,512]{0,1:T(8,128)(2,1)S(1)} %bitcast.229), channel_id=1, source_target_pairs={{0,3},{1,4},{2,5},{3,6},{4,7},{5,8},{6,9},{7,10},{8,11},{9,12},{10... | collective-permute-start | bytes 786440 | tf_op jit(solution)/shard_map/ppermute | solution.py:15
  17.4 27.1 %collective-permute-start.2 = (bf16[256,512]{1,0:T(8,128)(2,1)}, bf16[256,512]{1,0:T(8,128)(2,1)S(1)}, u32[]{:S(2)}, u32[]{:S(2)}) collective-permute-start(bf16[256,512]{1,0:T(8,128)(2,1)} %bitcast.238), channel_id=1, source_target_pairs={{0,1},{1,2},{2,3},{3,4},{4,5},{5,6},{6,7},{7,8},{8,9},{9,10},{10,1... | collective-permute-start | bytes 786440 | tf_op jit(solution)/shard_map/ppermute | solution.py:15
  20.0 37.6 %collective-permute-start.1 = (bf16[256,512]{1,0:T(8,128)(2,1)}, bf16[256,512]{1,0:T(8,128)(2,1)}, u32[]{:S(2)}, u32[]{:S(2)}) collective-permute-start(bf16[256,512]{1,0:T(8,128)(2,1)} %bitcast.239), channel_id=1, source_target_pairs={{0,2},{1,3},{2,4},{3,5},{4,6},{5,7},{6,8},{7,9},{8,10},{9,11},{10,... | collective-permute-start | bytes 786440 | tf_op jit(solution)/shard_map/ppermute | solution.py:15
  24.7 31.9 %copy-start = (f32[1,256,2560]{1,2,0:T(8,128)}, f32[1,256,2560]{1,2,0:T(8,128)S(1)}, u32[]{:S(2)}) copy-start(f32[1,256,2560]{1,2,0:T(8,128)S(1)} %copy.41) | copy-start | bytes 7864324
  24.7 1.8 copy-start.10
  24.7 19.7 %copy-start.7 = (bf16[1,256,512]{2,1,0:T(8,128)(2,1)S(1)}, bf16[1,256,512]{2,1,0:T(8,128)(2,1)}, u32[]{:S(2)}) copy-start(bf16[1,256,512]{2,1,0:T(8,128)(2,1)} %param.10) | copy-start | bytes 786436
  44.5 9.5 %copy-start.8 = (bf16[256,512]{1,0:T(8,128)(2,1)}, bf16[256,512]{1,0:T(8,128)(2,1)S(1)}, u32[]{:S(2)}) copy-start(bf16[256,512]{1,0:T(8,128)(2,1)S(1)} %collective-permute-done.2) | copy-start | bytes 786436
  44.5 16.7 %collective-permute-start = (bf16[256,512]{1,0:T(8,128)(2,1)S(1)}, bf16[256,512]{1,0:T(8,128)(2,1)}, u32[]{:S(2)}, u32[]{:S(2)}) collective-permute-start(bf16[256,512]{1,0:T(8,128)(2,1)S(1)} %bitcast.240), channel_id=1, source_target_pairs={{0,3},{1,4},{2,5},{3,6},{4,7},{5,8},{6,9},{7,10},{8,11},{9,12},{10... | collective-permute-start | bytes 786440 | tf_op jit(solution)/shard_map/ppermute | solution.py:15
  57.7 5.7 %copy-start.2 = (bf16[4,256,5,128]{1,3,2,0:T(8,128)(2,1)S(1)}, bf16[4,256,5,128]{1,3,2,0:T(8,128)(2,1)}, u32[]{:S(2)}) copy-start(bf16[4,256,5,128]{1,3,2,0:T(8,128)(2,1)} %fusion.35) | copy-start | bytes 3932164
  67.1 1.2 copy-start.5
  84.1 1.2 copy-start.5
  101.2 1.2 copy-start.5
  118.2 1.2 copy-start.5
  133.1 6.1 %copy-start.3 = (f32[4,256,5,128]{1,3,2,0:T(8,128)S(1)}, f32[4,256,5,128]{1,3,2,0:T(8,128)}, u32[]{:S(2)}) copy-start(f32[4,256,5,128]{1,3,2,0:T(8,128)} %get-tuple-element.61) | copy-start | bytes 7864324
  133.2 6.1 %copy-start.9 = (f32[2560]{0:T(1024)S(1)}, f32[2560]{0:T(1024)}, u32[]{:S(2)}) copy-start(f32[2560]{0:T(1024)} %param.12) | copy-start | bytes 30724
  134.7 5.0 %copy-start.4 = (f32[4,1024,128]{2,1,0:T(8,128)S(1)}, f32[4,1024,128]{2,1,0:T(8,128)}, u32[]{:S(2)}) copy-start(f32[4,1024,128]{2,1,0:T(8,128)} %get-tuple-element.62) | copy-start | bytes 6291460
  135.1 43.2 %collective-permute-start.11 = (f32[4,256,128]{2,0,1:T(4,128)S(1)}, f32[4,256,128]{2,0,1:T(4,128)S(1)}, u32[]{:S(2)}, u32[]{:S(2)}) collective-permute-start(f32[4,256,128]{2,0,1:T(4,128)S(1)} %bitcast.237), channel_id=1, source_target_pairs={{3,0},{4,1},{5,2},{6,3},{7,4},{8,5},{9,6},{10,7},{11,8},{12,9},{13... | collective-permute-start | bytes 1572872 | tf_op jit(solution)/shard_map/ppermute | solution.py:15
  136.5 306.2 %collective-permute-start.9 = (f32[4,256,128]{2,0,1:T(4,128)}, f32[4,256,128]{2,0,1:T(4,128)}, u32[]{:S(2)}, u32[]{:S(2)}) collective-permute-start(f32[4,256,128]{2,0,1:T(4,128)} %bitcast.170), channel_id=1, source_target_pairs={{1,0},{2,1},{3,2},{4,3},{5,4},{6,5},{7,6},{8,7},{9,8},{10,9},{11,1... | collective-permute-start | bytes 1572872 | tf_op jit(solution)/shard_map/ppermute | solution.py:15
  137.8 304.9 %collective-permute-start.10 = (f32[4,256,128]{2,0,1:T(4,128)S(1)}, f32[4,256,128]{2,0,1:T(4,128)}, u32[]{:S(2)}, u32[]{:S(2)}) collective-permute-start(f32[4,256,128]{2,0,1:T(4,128)S(1)} %bitcast.235), channel_id=1, source_target_pairs={{2,0},{3,1},{4,2},{5,3},{6,4},{7,5},{8,6},{9,7},{10,8},{11,9},{12,... | collective-permute-start | bytes 1572872 | tf_op jit(solution)/shard_map/ppermute | solution.py:15
  139.9 39.7 %copy-start.1 = (f32[1,256,2560]{1,2,0:T(8,128)S(1)}, f32[1,256,2560]{1,2,0:T(8,128)}, u32[]{:S(2)}) copy-start(f32[1,256,2560]{1,2,0:T(8,128)} %copy-done) | copy-start | bytes 7864324
  142.5 302.9 %collective-permute-start.8 = (f32[4,256,128]{2,0,1:T(4,128)}, f32[4,256,128]{2,0,1:T(4,128)}, u32[]{:S(2)}, u32[]{:S(2)}) collective-permute-start(f32[4,256,128]{2,0,1:T(4,128)} %bitcast.171), channel_id=1, source_target_pairs={{3,0},{4,1},{5,2},{6,3},{7,4},{8,5},{9,6},{10,7},{11,8},{12,9},{13... | collective-permute-start | bytes 1572872 | tf_op jit(solution)/shard_map/ppermute | solution.py:15
  143.8 301.6 %collective-permute-start.6 = (f32[4,256,128]{2,0,1:T(4,128)}, f32[4,256,128]{2,0,1:T(4,128)}, u32[]{:S(2)}, u32[]{:S(2)}) collective-permute-start(f32[4,256,128]{2,0,1:T(4,128)} %bitcast.173), channel_id=1, source_target_pairs={{1,0},{2,1},{3,2},{4,3},{5,4},{6,5},{7,6},{8,7},{9,8},{10,9},{11,1... | collective-permute-start | bytes 1572872 | tf_op jit(solution)/shard_map/ppermute | solution.py:15
  178.3 1.3 copy-start.6
  178.3 267.1 %collective-permute-start.7 = (f32[4,256,128]{2,0,1:T(4,128)S(1)}, f32[4,256,128]{2,0,1:T(4,128)}, u32[]{:S(2)}, u32[]{:S(2)}) collective-permute-start(f32[4,256,128]{2,0,1:T(4,128)S(1)} %bitcast.236), channel_id=1, source_target_pairs={{2,0},{3,1},{4,2},{5,3},{6,4},{7,5},{8,6},{9,7},{10,8},{11,9},{12,... | collective-permute-start | bytes 1572872 | tf_op jit(solution)/shard_map/ppermute | solution.py:15
